TPU v7x, 128 devices: a whole 4x4x4 slice. The times are simulated.
128 devices in a mesh: ctx: 16 (over x, y), tp: 8 (over z, core).
Axes of the slice: x: 4, y: 4, z: 4, core: 2. Of those that a mesh axis runs over, the one named last changes fastest.
Arguments:
- queries: bfloat16 [4096, 8192], P('ctx', 'tp'), may hold values from -160 to 160
- keys: bfloat16 [4096, 1024], P('ctx', 'tp'), may hold values from -4 to 4
- values: bfloat16 [4096, 1024], P('ctx', 'tp'), may hold values from -6 to 6
- positions: int32 [4096], P('ctx'), may hold values from 0 to 4095, as said below
- out_weight: bfloat16 [8192, 8192], P('tp'), may hold values from -0.5 to 0.5
Outputs:
- attn_out: bfloat16 [4096, 8192], P(('ctx', 'tp'))
Inputs may be any that keep to these rules, and one draw needn't show every extreme that they name: positions holds every number of 0 to 4095 once; it is made of 32 runs of 128 rows, each run holding ascending consecutive positions that start at a multiple of 128; the order of the runs is arbitrary.
All inputs are finite; a program needn't handle non-finite values.
Results may differ from a plain program's by a relative error of at most 0.015.
Values may be sent and summed in bfloat16 or wider, within the bound.
No kernel may reach another device: no remote copies, remote signals or barrier semaphores. Data moves between devices by JAX's collectives and lax.ppermute only.
A program may use at most 64 MiB of HBM per device.

v0:
```python
import jax
import jax.numpy as jnp
from jax import lax
from jax.sharding import PartitionSpec as P

HD = 128


def shifted(block, axis, distance):
    devices = range(lax.axis_size(axis))
    route = [((i - distance) % len(devices), i) for i in devices]
    return lax.ppermute(block, axis, route)


def attend(query_block, query_pos, key_block, value_block, key_pos):
    rows_q = query_block.shape[0]
    rows_k = key_block.shape[0]
    groups = key_block.shape[1] // HD
    repeat = query_block.shape[1] // (groups * HD)
    query_heads = query_block.reshape(rows_q, groups, repeat, HD)
    key_heads = key_block.reshape(rows_k, groups, HD)
    value_heads = value_block.reshape(rows_k, groups, HD)
    scores = jnp.einsum(
        "qgrd,kgd->grqk", query_heads, key_heads, preferred_element_type=jnp.float32
    ) * HD ** (-0.5)
    visible = key_pos[None, :] <= query_pos[:, None]
    scores = jnp.where(visible, scores, jnp.float32(-1e30))
    block_max = jnp.max(scores, axis=-1)
    weights = jnp.where(visible, jnp.exp(scores - block_max[..., None]), jnp.float32(0.0))
    block_total = jnp.sum(weights, axis=-1)
    summed = jnp.einsum(
        "grqk,kgd->qgrd",
        weights.astype(jnp.bfloat16),
        value_heads,
        preferred_element_type=jnp.float32,
    )
    scaled = summed / jnp.transpose(jnp.maximum(block_total, 1.0), (2, 0, 1))[..., None]
    block_out = lax.optimization_barrier(
        scaled.reshape(rows_q, groups * repeat * HD).astype(jnp.bfloat16)
    )
    return (
        block_out,
        block_max.reshape(groups * repeat, rows_q),
        block_total.reshape(groups * repeat, rows_q),
    )


def combine_parts(outputs, maxima, totals):
    overall = jnp.max(maxima, axis=0)
    weights = jnp.exp(maxima - overall[None]) * totals
    weights = weights / jnp.sum(weights, axis=0)[None]
    number, tok_rows, head_width = outputs.shape
    head_count = maxima.shape[1]
    spread = outputs.astype(jnp.float32).reshape(
        number, tok_rows, head_count, head_width // head_count
    )
    merged = jnp.sum(spread * jnp.transpose(weights, (0, 2, 1))[..., None], axis=0)
    return merged.reshape(tok_rows, head_width).astype(jnp.bfloat16)


def join_parts(first_part, later):
    return tuple(
        (
            jnp.concatenate([leading[None], trailing], axis=0)
            for leading, trailing in zip(first_part, later)
        )
    )


def attend_block(query_block, query_pos, key_block, value_block, key_pos):
    return attend(query_block, query_pos, key_block, value_block, key_pos)


def on_device(queries, keys, values, positions, out_weight):
    cycle_size = lax.axis_size("ctx")
    device = lax.axis_index("ctx")
    tok_rows = queries.shape[0]
    everywhere = lax.all_gather(positions, "ctx", axis=0, tiled=True)

    def block_positions(owner_index):
        return lax.dynamic_slice_in_dim(everywhere, owner_index * tok_rows, tok_rows, 0)

    first_part = attend_block(queries, positions, keys, values, positions)
    offsets = jnp.arange(1, cycle_size, dtype=jnp.int32)

    def advance_keys(visiting, offset):
        visiting = shifted(visiting, "ctx", 1)
        source = (device - offset) % cycle_size
        return (
            visiting,
            attend_block(queries, positions, visiting[0], visiting[1], block_positions(source)),
        )

    _, later = lax.scan(advance_keys, jnp.stack([keys, values]), offsets)
    outputs, maxima, totals = join_parts(first_part, later)
    merged = combine_parts(outputs, maxima, totals)
    return lax.psum_scatter(
        jnp.dot(merged, out_weight, preferred_element_type=jnp.float32).astype(jnp.bfloat16),
        "tp",
        scatter_dimension=0,
        tiled=True,
    )


def solution(mesh):
    return jax.shard_map(
        on_device,
        mesh=mesh,
        in_specs=(P("ctx", "tp"), P("ctx", "tp"), P("ctx", "tp"), P("ctx"), P("tp", None)),
        out_specs=P(("ctx", "tp"), None),
        check_vma=False,
    )
```

profile of v0, /device:TPU:0, one launch (start us, length us, event | category | flops | bytes accessed | tf_op | source)
XLA Modules:
  0.0 261.6 jit_solution(7151259834409543554)
XLA Ops:
  7.4 23.8 %all-gather = s32[16,1,256]{2,1,0:T(1,128)S(1)} all-gather(s32[1,1,256]{2,1,0:T(1,128)} %bitcast.178), channel_id=1, replica_groups=mesh['ctx'=16,'tp'=8] {'ctx'}, dimensions={0}, use_global_device_ids=true | all-gather | bytes 17408 | tf_op jit(solution)/shard_map/all_gather | solution.py:78
  31.2 1.6 fusion.23
  34.4 167.3 %while.18 = (s32[]{:T(128)}, bf16[2,256,128]{2,1,0:T(8,128)(2,1)S(1)}, bf16[15,256,1024]{1,2,0:T(8,128)(2,1)}, f32[15,8,256]{2,1,0:T(8,128)S(1)}, f32[15,8,256]{...) while((s32[]{:T(128)}, ...), condition=%wide.region_5.6_spmd, body=%wide.region_2.5_spmd.sunk | while | flops 275838976 | bytes 9654660 | solution.py:94
  34.4 1.2 collective-permute-start
  37.1 5.7 %collective-permute-done = bf16[2,256,128]{2,1,0:T(8,128)(2,1)S(1)} collective-permute-done((bf16[2,256,128]{2,1,0:T(8,128)(2,1)S(1)}, bf16[2,256,128]{2,1,0:T(8,128)(2,1)S(1)}, u32[]{:S(2)}, u32[]{:S(2)}) %collective-permute-start) | collective-permute-done | bytes 131104 | tf_op jit(solution)/shard_map/while/body/eval_jaxpr/ppermute | solution.py:12
  46.8 6.8 %collective-permute-done = bf16[2,256,128]{2,1,0:T(8,128)(2,1)S(1)} collective-permute-done((bf16[2,256,128]{2,1,0:T(8,128)(2,1)S(1)}, bf16[2,256,128]{2,1,0:T(8,128)(2,1)S(1)}, u32[]{:S(2)}, u32[]{:S(2)}) %collective-permute-start) | collective-permute-done | bytes 131104 | tf_op jit(solution)/shard_map/while/body/eval_jaxpr/ppermute | solution.py:12
  57.7 7.2 %collective-permute-done = bf16[2,256,128]{2,1,0:T(8,128)(2,1)S(1)} collective-permute-done((bf16[2,256,128]{2,1,0:T(8,128)(2,1)S(1)}, bf16[2,256,128]{2,1,0:T(8,128)(2,1)S(1)}, u32[]{:S(2)}, u32[]{:S(2)}) %collective-permute-start) | collective-permute-done | bytes 131104 | tf_op jit(solution)/shard_map/while/body/eval_jaxpr/ppermute | solution.py:12
  69.1 8.0 %collective-permute-done = bf16[2,256,128]{2,1,0:T(8,128)(2,1)S(1)} collective-permute-done((bf16[2,256,128]{2,1,0:T(8,128)(2,1)S(1)}, bf16[2,256,128]{2,1,0:T(8,128)(2,1)S(1)}, u32[]{:S(2)}, u32[]{:S(2)}) %collective-permute-start) | collective-permute-done | bytes 131104 | tf_op jit(solution)/shard_map/while/body/eval_jaxpr/ppermute | solution.py:12
  81.2 7.2 %collective-permute-done = bf16[2,256,128]{2,1,0:T(8,128)(2,1)S(1)} collective-permute-done((bf16[2,256,128]{2,1,0:T(8,128)(2,1)S(1)}, bf16[2,256,128]{2,1,0:T(8,128)(2,1)S(1)}, u32[]{:S(2)}, u32[]{:S(2)}) %collective-permute-start) | collective-permute-done | bytes 131104 | tf_op jit(solution)/shard_map/while/body/eval_jaxpr/ppermute | solution.py:12
  92.5 6.8 %collective-permute-done = bf16[2,256,128]{2,1,0:T(8,128)(2,1)S(1)} collective-permute-done((bf16[2,256,128]{2,1,0:T(8,128)(2,1)S(1)}, bf16[2,256,128]{2,1,0:T(8,128)(2,1)S(1)}, u32[]{:S(2)}, u32[]{:S(2)}) %collective-permute-start) | collective-permute-done | bytes 131104 | tf_op jit(solution)/shard_map/while/body/eval_jaxpr/ppermute | solution.py:12
  103.4 6.8 %collective-permute-done = bf16[2,256,128]{2,1,0:T(8,128)(2,1)S(1)} collective-permute-done((bf16[2,256,128]{2,1,0:T(8,128)(2,1)S(1)}, bf16[2,256,128]{2,1,0:T(8,128)(2,1)S(1)}, u32[]{:S(2)}, u32[]{:S(2)}) %collective-permute-start) | collective-permute-done | bytes 131104 | tf_op jit(solution)/shard_map/while/body/eval_jaxpr/ppermute | solution.py:12
  114.3 6.8 %collective-permute-done = bf16[2,256,128]{2,1,0:T(8,128)(2,1)S(1)} collective-permute-done((bf16[2,256,128]{2,1,0:T(8,128)(2,1)S(1)}, bf16[2,256,128]{2,1,0:T(8,128)(2,1)S(1)}, u32[]{:S(2)}, u32[]{:S(2)}) %collective-permute-start) | collective-permute-done | bytes 131104 | tf_op jit(solution)/shard_map/while/body/eval_jaxpr/ppermute | solution.py:12
  125.2 6.8 %collective-permute-done = bf16[2,256,128]{2,1,0:T(8,128)(2,1)S(1)} collective-permute-done((bf16[2,256,128]{2,1,0:T(8,128)(2,1)S(1)}, bf16[2,256,128]{2,1,0:T(8,128)(2,1)S(1)}, u32[]{:S(2)}, u32[]{:S(2)}) %collective-permute-start) | collective-permute-done | bytes 131104 | tf_op jit(solution)/shard_map/while/body/eval_jaxpr/ppermute | solution.py:12
  136.1 6.8 %collective-permute-done = bf16[2,256,128]{2,1,0:T(8,128)(2,1)S(1)} collective-permute-done((bf16[2,256,128]{2,1,0:T(8,128)(2,1)S(1)}, bf16[2,256,128]{2,1,0:T(8,128)(2,1)S(1)}, u32[]{:S(2)}, u32[]{:S(2)}) %collective-permute-start) | collective-permute-done | bytes 131104 | tf_op jit(solution)/shard_map/while/body/eval_jaxpr/ppermute | solution.py:12
  144.6 0.9 bitcast_dynamic-update-slice_fusion.6
  147.0 6.8 %collective-permute-done = bf16[2,256,128]{2,1,0:T(8,128)(2,1)S(1)} collective-permute-done((bf16[2,256,128]{2,1,0:T(8,128)(2,1)S(1)}, bf16[2,256,128]{2,1,0:T(8,128)(2,1)S(1)}, u32[]{:S(2)}, u32[]{:S(2)}) %collective-permute-start) | collective-permute-done | bytes 131104 | tf_op jit(solution)/shard_map/while/body/eval_jaxpr/ppermute | solution.py:12
  157.9 7.3 %collective-permute-done = bf16[2,256,128]{2,1,0:T(8,128)(2,1)S(1)} collective-permute-done((bf16[2,256,128]{2,1,0:T(8,128)(2,1)S(1)}, bf16[2,256,128]{2,1,0:T(8,128)(2,1)S(1)}, u32[]{:S(2)}, u32[]{:S(2)}) %collective-permute-start) | collective-permute-done | bytes 131104 | tf_op jit(solution)/shard_map/while/body/eval_jaxpr/ppermute | solution.py:12
  169.3 8.1 %collective-permute-done = bf16[2,256,128]{2,1,0:T(8,128)(2,1)S(1)} collective-permute-done((bf16[2,256,128]{2,1,0:T(8,128)(2,1)S(1)}, bf16[2,256,128]{2,1,0:T(8,128)(2,1)S(1)}, u32[]{:S(2)}, u32[]{:S(2)}) %collective-permute-start) | collective-permute-done | bytes 131104 | tf_op jit(solution)/shard_map/while/body/eval_jaxpr/ppermute | solution.py:12
  181.4 6.8 %collective-permute-done = bf16[2,256,128]{2,1,0:T(8,128)(2,1)S(1)} collective-permute-done((bf16[2,256,128]{2,1,0:T(8,128)(2,1)S(1)}, bf16[2,256,128]{2,1,0:T(8,128)(2,1)S(1)}, u32[]{:S(2)}, u32[]{:S(2)}) %collective-permute-start) | collective-permute-done | bytes 131104 | tf_op jit(solution)/shard_map/while/body/eval_jaxpr/ppermute | solution.py:12
  189.9 0.9 bitcast_dynamic-update-slice_fusion.6
  192.3 6.8 %collective-permute-done = bf16[2,256,128]{2,1,0:T(8,128)(2,1)S(1)} collective-permute-done((bf16[2,256,128]{2,1,0:T(8,128)(2,1)S(1)}, bf16[2,256,128]{2,1,0:T(8,128)(2,1)S(1)}, u32[]{:S(2)}, u32[]{:S(2)}) %collective-permute-start) | collective-permute-done | bytes 131104 | tf_op jit(solution)/shard_map/while/body/eval_jaxpr/ppermute | solution.py:12
  201.8 5.2 %multiply_reduce_fusion = bf16[256,8,128]{0,2,1:T(8,128)(2,1)S(1)} fusion(bf16[15,256,8,128]{1,3,2,0:T(8,128)(2,1)} %bitcast.170, bf16[1,256,8,128]{1,3,2,0:T(8,128)(2,1)S(1)} %bitcast.172, f32[16,256,8]{1,2,0:T(8,128)S(1)} %divide_bitcast_fusion), kind=kLoop, calls=%fused_computation.28 | loop fusion | flops 24903680 | bytes 9043968 | tf_op jit(solution)/shard_map/reduce_sum | solution.py:57
  207.0 12.0 %convolution_convert_fusion = bf16[256,8192]{1,0:T(8,128)(2,1)} fusion(bf16[256,1024]{0,1:T(8,128)(2,1)S(1)} %bitcast.171, bf16[1024,8192]{1,0:T(8,128)(2,1)} %param.11), kind=kOutput, calls=%fused_computation.29 | convolution fusion | flops 4297064448 | bytes 21495808 | tf_op jit(solution)/shard_map/dot_general | solution.py:98
  219.1 35.7 %reduce-scatter.2.cloned.1.call-done = bf16[32,8192]{1,0:T(8,128)(2,1)} async-done(((bf16[256,8192]{1,0:T(8,128)(2,1)}), bf16[32,8192]{1,0:T(8,128)(2,1)}) %reduce-scatter.2.cloned.1.call-update) | async-done | bytes 524304 | tf_op jit(solution)/shard_map/reduce_scatter | solution.py:97
  (170 shorter events, 51.0 us)
Async XLA Ops:
  6.5 248.2 %reduce-scatter.2.cloned.1.call-start = ((), (), s32[]{:S(2)}) async-start(), calls=%async_computation.1 | async-start | bytes 4718592 | tf_op jit(solution)/shard_map/reduce_scatter | solution.py:97
  31.2 2.1 copy-start.3
  33.3 0.8 copy-start.1
  33.4 1.1 copy-start
  33.4 1.1 copy-start.2
  34.4 8.3 %collective-permute-start = (bf16[2,256,128]{2,1,0:T(8,128)(2,1)S(1)}, bf16[2,256,128]{2,1,0:T(8,128)(2,1)S(1)}, u32[]{:S(2)}, u32[]{:S(2)}) collective-permute-start(bf16[2,256,128]{2,1,0:T(8,128)(2,1)S(1)} %get-tuple-element.251), channel_id=1, source_target_pairs={{120,0},{0,8},{8,16},{16,24},{24,32},{32,40},{40,48},{48,56},{56,6... | collective-permute-start | bytes 393224 | tf_op jit(solution)/shard_map/while/body/eval_jaxpr/ppermute | solution.py:12
  45.3 8.4 %collective-permute-start = (bf16[2,256,128]{2,1,0:T(8,128)(2,1)S(1)}, bf16[2,256,128]{2,1,0:T(8,128)(2,1)S(1)}, u32[]{:S(2)}, u32[]{:S(2)}) collective-permute-start(bf16[2,256,128]{2,1,0:T(8,128)(2,1)S(1)} %get-tuple-element.251), channel_id=1, source_target_pairs={{120,0},{0,8},{8,16},{16,24},{24,32},{32,40},{40,48},{48,56},{56,6... | collective-permute-start | bytes 393224 | tf_op jit(solution)/shard_map/while/body/eval_jaxpr/ppermute | solution.py:12
  56.2 8.8 %collective-permute-start = (bf16[2,256,128]{2,1,0:T(8,128)(2,1)S(1)}, bf16[2,256,128]{2,1,0:T(8,128)(2,1)S(1)}, u32[]{:S(2)}, u32[]{:S(2)}) collective-permute-start(bf16[2,256,128]{2,1,0:T(8,128)(2,1)S(1)} %get-tuple-element.251), channel_id=1, source_target_pairs={{120,0},{0,8},{8,16},{16,24},{24,32},{32,40},{40,48},{48,56},{56,6... | collective-permute-start | bytes 393224 | tf_op jit(solution)/shard_map/while/body/eval_jaxpr/ppermute | solution.py:12
  67.5 9.6 %collective-permute-start = (bf16[2,256,128]{2,1,0:T(8,128)(2,1)S(1)}, bf16[2,256,128]{2,1,0:T(8,128)(2,1)S(1)}, u32[]{:S(2)}, u32[]{:S(2)}) collective-permute-start(bf16[2,256,128]{2,1,0:T(8,128)(2,1)S(1)} %get-tuple-element.251), channel_id=1, source_target_pairs={{120,0},{0,8},{8,16},{16,24},{24,32},{32,40},{40,48},{48,56},{56,6... | collective-permute-start | bytes 393224 | tf_op jit(solution)/shard_map/while/body/eval_jaxpr/ppermute | solution.py:12
  79.7 8.7 %collective-permute-start = (bf16[2,256,128]{2,1,0:T(8,128)(2,1)S(1)}, bf16[2,256,128]{2,1,0:T(8,128)(2,1)S(1)}, u32[]{:S(2)}, u32[]{:S(2)}) collective-permute-start(bf16[2,256,128]{2,1,0:T(8,128)(2,1)S(1)} %get-tuple-element.251), channel_id=1, source_target_pairs={{120,0},{0,8},{8,16},{16,24},{24,32},{32,40},{40,48},{48,56},{56,6... | collective-permute-start | bytes 393224 | tf_op jit(solution)/shard_map/while/body/eval_jaxpr/ppermute | solution.py:12
  90.9 8.4 %collective-permute-start = (bf16[2,256,128]{2,1,0:T(8,128)(2,1)S(1)}, bf16[2,256,128]{2,1,0:T(8,128)(2,1)S(1)}, u32[]{:S(2)}, u32[]{:S(2)}) collective-permute-start(bf16[2,256,128]{2,1,0:T(8,128)(2,1)S(1)} %get-tuple-element.251), channel_id=1, source_target_pairs={{120,0},{0,8},{8,16},{16,24},{24,32},{32,40},{40,48},{48,56},{56,6... | collective-permute-start | bytes 393224 | tf_op jit(solution)/shard_map/while/body/eval_jaxpr/ppermute | solution.py:12
  101.8 8.4 %collective-permute-start = (bf16[2,256,128]{2,1,0:T(8,128)(2,1)S(1)}, bf16[2,256,128]{2,1,0:T(8,128)(2,1)S(1)}, u32[]{:S(2)}, u32[]{:S(2)}) collective-permute-start(bf16[2,256,128]{2,1,0:T(8,128)(2,1)S(1)} %get-tuple-element.251), channel_id=1, source_target_pairs={{120,0},{0,8},{8,16},{16,24},{24,32},{32,40},{40,48},{48,56},{56,6... | collective-permute-start | bytes 393224 | tf_op jit(solution)/shard_map/while/body/eval_jaxpr/ppermute | solution.py:12
  112.7 8.4 %collective-permute-start = (bf16[2,256,128]{2,1,0:T(8,128)(2,1)S(1)}, bf16[2,256,128]{2,1,0:T(8,128)(2,1)S(1)}, u32[]{:S(2)}, u32[]{:S(2)}) collective-permute-start(bf16[2,256,128]{2,1,0:T(8,128)(2,1)S(1)} %get-tuple-element.251), channel_id=1, source_target_pairs={{120,0},{0,8},{8,16},{16,24},{24,32},{32,40},{40,48},{48,56},{56,6... | collective-permute-start | bytes 393224 | tf_op jit(solution)/shard_map/while/body/eval_jaxpr/ppermute | solution.py:12
  123.7 8.4 %collective-permute-start = (bf16[2,256,128]{2,1,0:T(8,128)(2,1)S(1)}, bf16[2,256,128]{2,1,0:T(8,128)(2,1)S(1)}, u32[]{:S(2)}, u32[]{:S(2)}) collective-permute-start(bf16[2,256,128]{2,1,0:T(8,128)(2,1)S(1)} %get-tuple-element.251), channel_id=1, source_target_pairs={{120,0},{0,8},{8,16},{16,24},{24,32},{32,40},{40,48},{48,56},{56,6... | collective-permute-start | bytes 393224 | tf_op jit(solution)/shard_map/while/body/eval_jaxpr/ppermute | solution.py:12
  134.5 8.4 %collective-permute-start = (bf16[2,256,128]{2,1,0:T(8,128)(2,1)S(1)}, bf16[2,256,128]{2,1,0:T(8,128)(2,1)S(1)}, u32[]{:S(2)}, u32[]{:S(2)}) collective-permute-start(bf16[2,256,128]{2,1,0:T(8,128)(2,1)S(1)} %get-tuple-element.251), channel_id=1, source_target_pairs={{120,0},{0,8},{8,16},{16,24},{24,32},{32,40},{40,48},{48,56},{56,6... | collective-permute-start | bytes 393224 | tf_op jit(solution)/shard_map/while/body/eval_jaxpr/ppermute | solution.py:12
  145.5 8.4 %collective-permute-start = (bf16[2,256,128]{2,1,0:T(8,128)(2,1)S(1)}, bf16[2,256,128]{2,1,0:T(8,128)(2,1)S(1)}, u32[]{:S(2)}, u32[]{:S(2)}) collective-permute-start(bf16[2,256,128]{2,1,0:T(8,128)(2,1)S(1)} %get-tuple-element.251), channel_id=1, source_target_pairs={{120,0},{0,8},{8,16},{16,24},{24,32},{32,40},{40,48},{48,56},{56,6... | collective-permute-start | bytes 393224 | tf_op jit(solution)/shard_map/while/body/eval_jaxpr/ppermute | solution.py:12
  156.4 8.8 %collective-permute-start = (bf16[2,256,128]{2,1,0:T(8,128)(2,1)S(1)}, bf16[2,256,128]{2,1,0:T(8,128)(2,1)S(1)}, u32[]{:S(2)}, u32[]{:S(2)}) collective-permute-start(bf16[2,256,128]{2,1,0:T(8,128)(2,1)S(1)} %get-tuple-element.251), channel_id=1, source_target_pairs={{120,0},{0,8},{8,16},{16,24},{24,32},{32,40},{40,48},{48,56},{56,6... | collective-permute-start | bytes 393224 | tf_op jit(solution)/shard_map/while/body/eval_jaxpr/ppermute | solution.py:12
  167.7 9.6 %collective-permute-start = (bf16[2,256,128]{2,1,0:T(8,128)(2,1)S(1)}, bf16[2,256,128]{2,1,0:T(8,128)(2,1)S(1)}, u32[]{:S(2)}, u32[]{:S(2)}) collective-permute-start(bf16[2,256,128]{2,1,0:T(8,128)(2,1)S(1)} %get-tuple-element.251), channel_id=1, source_target_pairs={{120,0},{0,8},{8,16},{16,24},{24,32},{32,40},{40,48},{48,56},{56,6... | collective-permute-start | bytes 393224 | tf_op jit(solution)/shard_map/while/body/eval_jaxpr/ppermute | solution.py:12
  179.9 8.4 %collective-permute-start = (bf16[2,256,128]{2,1,0:T(8,128)(2,1)S(1)}, bf16[2,256,128]{2,1,0:T(8,128)(2,1)S(1)}, u32[]{:S(2)}, u32[]{:S(2)}) collective-permute-start(bf16[2,256,128]{2,1,0:T(8,128)(2,1)S(1)} %get-tuple-element.251), channel_id=1, source_target_pairs={{120,0},{0,8},{8,16},{16,24},{24,32},{32,40},{40,48},{48,56},{56,6... | collective-permute-start | bytes 393224 | tf_op jit(solution)/shard_map/while/body/eval_jaxpr/ppermute | solution.py:12
  190.8 8.4 %collective-permute-start = (bf16[2,256,128]{2,1,0:T(8,128)(2,1)S(1)}, bf16[2,256,128]{2,1,0:T(8,128)(2,1)S(1)}, u32[]{:S(2)}, u32[]{:S(2)}) collective-permute-start(bf16[2,256,128]{2,1,0:T(8,128)(2,1)S(1)} %get-tuple-element.251), channel_id=1, source_target_pairs={{120,0},{0,8},{8,16},{16,24},{24,32},{32,40},{40,48},{48,56},{56,6... | collective-permute-start | bytes 393224 | tf_op jit(solution)/shard_map/while/body/eval_jaxpr/ppermute | solution.py:12
Sparse Core Ops, SparseCore 0:
  219.2 35.5 reduce-scatter.1
where the time goes:
time: 262 us
  waiting for transfers between devices  140 us (53%)
  matrix products  31.2 us (12%)
  blocking collectives  23.8 us (9%)
  local copies, waits for them, and re-layouts  23.2 us (9%)
  other arithmetic  16.1 us (6%)
  between operations  13.5 us (5%)
  loops' own time  11 us (4%)
    ppermute x15, waiting for transfers between devices, shifted(): return lax.ppermute(block, axis, route)  105 us
    reduce_scatter x1, waiting for transfers between devices, on_device(): lax.psum_scatter(jnp.dot(merged, out_weight, preferred_element_type=jnp.f...  35.7 us
    all_gather x1, blocking collectives, on_device(): everywhere = lax.all_gather(positions, 'ctx', axis=0, tiled=True)  23.8 us
    dynamic_update_slice x15, local copies, waits for them, and re-layouts, on_device(): _, later = lax.scan(advance_keys, jnp.stack([keys, values]), offsets)  12.7 us
    dot_general x1, matrix products, on_device(): jnp.dot(merged, out_weight, preferred_element_type=jnp.float32)  12 us
    another operation x1, loops' own time, on_device(): _, later = lax.scan(advance_keys, jnp.stack([keys, values]), offsets)  11 us
    dot_general x16, matrix products, attend(): jnp.einsum('grqk,kgd->qgrd', weights.astype(jnp.bfloat16), value_heads, p...  10.4 us
    dynamic_slice x15, local copies, waits for them, and re-layouts, on_device(): _, later = lax.scan(advance_keys, jnp.stack([keys, values]), offsets)  8.83 us
  transfers between devices with their start and end apart: 16, of which 16 were waited for; matrix products, arithmetic and copies ran while one was open for 4% of the time, Pallas kernels for 0%

commit v1 on v0

--- a/solution.py
+++ b/solution.py
@@ -75,7 +75,9 @@
     cycle_size = lax.axis_size("ctx")
     device = lax.axis_index("ctx")
     tok_rows = queries.shape[0]
-    everywhere = lax.all_gather(positions, "ctx", axis=0, tiled=True)
+    everywhere = jnp.concatenate(
+        lax.all_to_all(jnp.stack([positions] * lax.axis_size("ctx")), "ctx", 0, 0), axis=0
+    )
 
     def block_positions(owner_index):
         return lax.dynamic_slice_in_dim(everywhere, owner_index * tok_rows, tok_rows, 0)

time: 262 us -> 248 us (0.947)
  blocking collectives: 23.8 us -> 0 us
  starting transfers between devices: 2.24 us -> 8.8 us
  waiting for transfers between devices: 140 us -> 143 us
    all_gather x1 -> x0, blocking collectives: 23.8 us -> none  [on_device(): everywhere = lax.all_gather(positions, 'ctx', axis=0, tiled=True)]
    all_to_all x0 -> x1, starting transfers between devices: none -> 7.15 us  [on_device(): lax.all_to_all(jnp.stack([positions] * lax.axis_size('ctx')), 'ctx', 0, 0)]
    all_to_all x0 -> x1, waiting for transfers between devices: none -> 3.63 us  [on_device(): lax.all_to_all(jnp.stack([positions] * lax.axis_size('ctx')), 'ctx', 0, 0)]
  transfers between devices with their start and end apart: 16 -> 17, of which waited for: 16 -> 17; matrix products, arithmetic and copies ran while one was open for 4% -> 6% of each run, Pallas kernels for 0% -> 0%
where the time goes in v1:
time: 248 us
  waiting for transfers between devices  143 us (58%)
  matrix products  31.2 us (13%)
  local copies, waits for them, and re-layouts  24.3 us (10%)
  other arithmetic  16.1 us (6%)
  between operations  13.6 us (5%)
  loops' own time  11 us (4%)
  starting transfers between devices  8.8 us (4%)
    ppermute x15, waiting for transfers between devices, shifted(): return lax.ppermute(block, axis, route)  103 us
    reduce_scatter x1, waiting for transfers between devices, on_device(): lax.psum_scatter(jnp.dot(merged, out_weight, preferred_element_type=jnp.f...  35.6 us
    dynamic_update_slice x15, local copies, waits for them, and re-layouts, on_device(): _, later = lax.scan(advance_keys, jnp.stack([keys, values]), offsets)  12.7 us
    dot_general x1, matrix products, on_device(): jnp.dot(merged, out_weight, preferred_element_type=jnp.float32)  12 us
    another operation x1, loops' own time, on_device(): _, later = lax.scan(advance_keys, jnp.stack([keys, values]), offsets)  11 us
    dot_general x16, matrix products, attend(): jnp.einsum('grqk,kgd->qgrd', weights.astype(jnp.bfloat16), value_heads, p...  10.4 us
    dynamic_slice x15, local copies, waits for them, and re-layouts, on_device(): _, later = lax.scan(advance_keys, jnp.stack([keys, values]), offsets)  8.83 us
    dot_general x16, matrix products, attend(): jnp.einsum('qgrd,kgd->grqk', query_heads, key_heads, preferred_element_ty...  8.72 us
  transfers between devices with their start and end apart: 17, of which 17 were waited for; matrix products, arithmetic and copies ran while one was open for 6% of the time, Pallas kernels for 0%

profile of v1, /device:TPU:0, one launch (start us, length us, event | category | flops | bytes accessed | tf_op | source)
XLA Modules:
  0.0 247.7 jit_solution(13682648855842971457)
XLA Ops:
  6.5 1.3 stack.11
  7.8 7.1 %all-to-all-start = ((s32[16,1,256]{2,1,0:T(1,128)}), s32[16,1,256]{2,1,0:T(1,128)S(1)}, u32[]{:S(2)}, u32[]{:S(2)}) async-start(s32[16,1,256]{2,1,0:T(1,128)} %stack.11), calls=%async_computation | async-start | bytes 32768 | tf_op jit(solution)/shard_map/all_to_all | solution.py:79
  15.9 1.6 fusion.23
  18.9 3.6 %all-to-all-done = s32[16,1,256]{2,1,0:T(1,128)S(1)} async-done(((s32[16,1,256]{2,1,0:T(1,128)}), s32[16,1,256]{2,1,0:T(1,128)S(1)}, u32[]{:S(2)}, u32[]{:S(2)}) %all-to-all-start) | async-done | bytes 16416 | tf_op jit(solution)/shard_map/all_to_all | solution.py:79
  22.6 165.3 %while.18 = (s32[]{:T(128)}, bf16[2,256,128]{2,1,0:T(8,128)(2,1)S(1)}, bf16[15,256,1024]{1,2,0:T(8,128)(2,1)}, f32[15,8,256]{2,1,0:T(8,128)S(1)}, f32[15,8,256]{...) while((s32[]{:T(128)}, ...), condition=%wide.region_5.6_spmd, body=%wide.region_2.5_spmd.sunk | while | flops 275838976 | bytes 9654660 | solution.py:96
  24.6 6.3 %collective-permute-done = bf16[2,256,128]{2,1,0:T(8,128)(2,1)S(1)} collective-permute-done((bf16[2,256,128]{2,1,0:T(8,128)(2,1)S(1)}, bf16[2,256,128]{2,1,0:T(8,128)(2,1)S(1)}, u32[]{:S(2)}, u32[]{:S(2)}) %collective-permute-start) | collective-permute-done | bytes 131104 | tf_op jit(solution)/shard_map/while/body/eval_jaxpr/ppermute | solution.py:12
  35.0 6.8 %collective-permute-done = bf16[2,256,128]{2,1,0:T(8,128)(2,1)S(1)} collective-permute-done((bf16[2,256,128]{2,1,0:T(8,128)(2,1)S(1)}, bf16[2,256,128]{2,1,0:T(8,128)(2,1)S(1)}, u32[]{:S(2)}, u32[]{:S(2)}) %collective-permute-start) | collective-permute-done | bytes 131104 | tf_op jit(solution)/shard_map/while/body/eval_jaxpr/ppermute | solution.py:12
  45.9 6.8 %collective-permute-done = bf16[2,256,128]{2,1,0:T(8,128)(2,1)S(1)} collective-permute-done((bf16[2,256,128]{2,1,0:T(8,128)(2,1)S(1)}, bf16[2,256,128]{2,1,0:T(8,128)(2,1)S(1)}, u32[]{:S(2)}, u32[]{:S(2)}) %collective-permute-start) | collective-permute-done | bytes 131104 | tf_op jit(solution)/shard_map/while/body/eval_jaxpr/ppermute | solution.py:12
  56.8 6.8 %collective-permute-done = bf16[2,256,128]{2,1,0:T(8,128)(2,1)S(1)} collective-permute-done((bf16[2,256,128]{2,1,0:T(8,128)(2,1)S(1)}, bf16[2,256,128]{2,1,0:T(8,128)(2,1)S(1)}, u32[]{:S(2)}, u32[]{:S(2)}) %collective-permute-start) | collective-permute-done | bytes 131104 | tf_op jit(solution)/shard_map/while/body/eval_jaxpr/ppermute | solution.py:12
  67.7 6.8 %collective-permute-done = bf16[2,256,128]{2,1,0:T(8,128)(2,1)S(1)} collective-permute-done((bf16[2,256,128]{2,1,0:T(8,128)(2,1)S(1)}, bf16[2,256,128]{2,1,0:T(8,128)(2,1)S(1)}, u32[]{:S(2)}, u32[]{:S(2)}) %collective-permute-start) | collective-permute-done | bytes 131104 | tf_op jit(solution)/shard_map/while/body/eval_jaxpr/ppermute | solution.py:12
  78.6 6.8 %collective-permute-done = bf16[2,256,128]{2,1,0:T(8,128)(2,1)S(1)} collective-permute-done((bf16[2,256,128]{2,1,0:T(8,128)(2,1)S(1)}, bf16[2,256,128]{2,1,0:T(8,128)(2,1)S(1)}, u32[]{:S(2)}, u32[]{:S(2)}) %collective-permute-start) | collective-permute-done | bytes 131104 | tf_op jit(solution)/shard_map/while/body/eval_jaxpr/ppermute | solution.py:12
  89.5 7.9 %collective-permute-done = bf16[2,256,128]{2,1,0:T(8,128)(2,1)S(1)} collective-permute-done((bf16[2,256,128]{2,1,0:T(8,128)(2,1)S(1)}, bf16[2,256,128]{2,1,0:T(8,128)(2,1)S(1)}, u32[]{:S(2)}, u32[]{:S(2)}) %collective-permute-start) | collective-permute-done | bytes 131104 | tf_op jit(solution)/shard_map/while/body/eval_jaxpr/ppermute | solution.py:12
  101.5 7.4 %collective-permute-done = bf16[2,256,128]{2,1,0:T(8,128)(2,1)S(1)} collective-permute-done((bf16[2,256,128]{2,1,0:T(8,128)(2,1)S(1)}, bf16[2,256,128]{2,1,0:T(8,128)(2,1)S(1)}, u32[]{:S(2)}, u32[]{:S(2)}) %collective-permute-start) | collective-permute-done | bytes 131104 | tf_op jit(solution)/shard_map/while/body/eval_jaxpr/ppermute | solution.py:12
  113.0 6.8 %collective-permute-done = bf16[2,256,128]{2,1,0:T(8,128)(2,1)S(1)} collective-permute-done((bf16[2,256,128]{2,1,0:T(8,128)(2,1)S(1)}, bf16[2,256,128]{2,1,0:T(8,128)(2,1)S(1)}, u32[]{:S(2)}, u32[]{:S(2)}) %collective-permute-start) | collective-permute-done | bytes 131104 | tf_op jit(solution)/shard_map/while/body/eval_jaxpr/ppermute | solution.py:12
  123.9 6.8 %collective-permute-done = bf16[2,256,128]{2,1,0:T(8,128)(2,1)S(1)} collective-permute-done((bf16[2,256,128]{2,1,0:T(8,128)(2,1)S(1)}, bf16[2,256,128]{2,1,0:T(8,128)(2,1)S(1)}, u32[]{:S(2)}, u32[]{:S(2)}) %collective-permute-start) | collective-permute-done | bytes 131104 | tf_op jit(solution)/shard_map/while/body/eval_jaxpr/ppermute | solution.py:12
  134.9 6.8 %collective-permute-done = bf16[2,256,128]{2,1,0:T(8,128)(2,1)S(1)} collective-permute-done((bf16[2,256,128]{2,1,0:T(8,128)(2,1)S(1)}, bf16[2,256,128]{2,1,0:T(8,128)(2,1)S(1)}, u32[]{:S(2)}, u32[]{:S(2)}) %collective-permute-start) | collective-permute-done | bytes 131104 | tf_op jit(solution)/shard_map/while/body/eval_jaxpr/ppermute | solution.py:12
  145.8 6.8 %collective-permute-done = bf16[2,256,128]{2,1,0:T(8,128)(2,1)S(1)} collective-permute-done((bf16[2,256,128]{2,1,0:T(8,128)(2,1)S(1)}, bf16[2,256,128]{2,1,0:T(8,128)(2,1)S(1)}, u32[]{:S(2)}, u32[]{:S(2)}) %collective-permute-start) | collective-permute-done | bytes 131104 | tf_op jit(solution)/shard_map/while/body/eval_jaxpr/ppermute | solution.py:12
  156.7 6.8 %collective-permute-done = bf16[2,256,128]{2,1,0:T(8,128)(2,1)S(1)} collective-permute-done((bf16[2,256,128]{2,1,0:T(8,128)(2,1)S(1)}, bf16[2,256,128]{2,1,0:T(8,128)(2,1)S(1)}, u32[]{:S(2)}, u32[]{:S(2)}) %collective-permute-start) | collective-permute-done | bytes 131104 | tf_op jit(solution)/shard_map/while/body/eval_jaxpr/ppermute | solution.py:12
  167.6 6.8 %collective-permute-done = bf16[2,256,128]{2,1,0:T(8,128)(2,1)S(1)} collective-permute-done((bf16[2,256,128]{2,1,0:T(8,128)(2,1)S(1)}, bf16[2,256,128]{2,1,0:T(8,128)(2,1)S(1)}, u32[]{:S(2)}, u32[]{:S(2)}) %collective-permute-start) | collective-permute-done | bytes 131104 | tf_op jit(solution)/shard_map/while/body/eval_jaxpr/ppermute | solution.py:12
  176.1 0.9 bitcast_dynamic-update-slice_fusion.6
  178.5 6.8 %collective-permute-done = bf16[2,256,128]{2,1,0:T(8,128)(2,1)S(1)} collective-permute-done((bf16[2,256,128]{2,1,0:T(8,128)(2,1)S(1)}, bf16[2,256,128]{2,1,0:T(8,128)(2,1)S(1)}, u32[]{:S(2)}, u32[]{:S(2)}) %collective-permute-start) | collective-permute-done | bytes 131104 | tf_op jit(solution)/shard_map/while/body/eval_jaxpr/ppermute | solution.py:12
  188.0 5.2 %multiply_reduce_fusion = bf16[256,8,128]{0,2,1:T(8,128)(2,1)S(1)} fusion(bf16[15,256,8,128]{1,3,2,0:T(8,128)(2,1)} %bitcast.169, bf16[1,256,8,128]{1,3,2,0:T(8,128)(2,1)S(1)} %bitcast.171, f32[16,256,8]{1,2,0:T(8,128)S(1)} %divide_bitcast_fusion), kind=kLoop, calls=%fused_computation.28 | loop fusion | flops 24903680 | bytes 9043968 | tf_op jit(solution)/shard_map/reduce_sum | solution.py:57
  193.2 12.0 %convolution_convert_fusion = bf16[256,8192]{1,0:T(8,128)(2,1)} fusion(bf16[256,1024]{0,1:T(8,128)(2,1)S(1)} %bitcast.170, bf16[1024,8192]{1,0:T(8,128)(2,1)} %param.11), kind=kOutput, calls=%fused_computation.29 | convolution fusion | flops 4297064448 | bytes 21495808 | tf_op jit(solution)/shard_map/dot_general | solution.py:100
  205.2 35.6 %reduce-scatter.2.cloned.1.call-done = bf16[32,8192]{1,0:T(8,128)(2,1)} async-done(((bf16[256,8192]{1,0:T(8,128)(2,1)}), bf16[32,8192]{1,0:T(8,128)(2,1)}) %reduce-scatter.2.cloned.1.call-update) | async-done | bytes 524304 | tf_op jit(solution)/shard_map/reduce_scatter | solution.py:99
  (172 shorter events, 52.3 us)
Async XLA Ops:
  7.8 14.8 %all-to-all-start = ((s32[16,1,256]{2,1,0:T(1,128)}), s32[16,1,256]{2,1,0:T(1,128)S(1)}, u32[]{:S(2)}, u32[]{:S(2)}) async-start(s32[16,1,256]{2,1,0:T(1,128)} %stack.11), calls=%async_computation | async-start | bytes 32768 | tf_op jit(solution)/shard_map/all_to_all | solution.py:79
  15.0 225.9 %reduce-scatter.2.cloned.1.call-start = ((), (), s32[]{:S(2)}) async-start(), calls=%async_computation.2 | async-start | bytes 4718592 | tf_op jit(solution)/shard_map/reduce_scatter | solution.py:99
  15.9 2.1 copy-start.3
  18.0 0.8 copy-start.1
  18.1 4.5 %copy-start = (bf16[256,1024]{1,0:T(8,128)(2,1)S(1)}, bf16[256,1024]{1,0:T(8,128)(2,1)}, u32[]{:S(2)}) copy-start(bf16[256,1024]{1,0:T(8,128)(2,1)} %param.7) | copy-start | bytes 1572868
  18.1 4.5 %copy-start.2 = (s32[256]{0:T(256)S(1)}, s32[256]{0:T(256)}, u32[]{:S(2)}) copy-start(s32[256]{0:T(256)} %param.10) | copy-start | bytes 3076
  22.6 8.3 %collective-permute-start = (bf16[2,256,128]{2,1,0:T(8,128)(2,1)S(1)}, bf16[2,256,128]{2,1,0:T(8,128)(2,1)S(1)}, u32[]{:S(2)}, u32[]{:S(2)}) collective-permute-start(bf16[2,256,128]{2,1,0:T(8,128)(2,1)S(1)} %get-tuple-element.251), channel_id=1, source_target_pairs={{120,0},{0,8},{8,16},{16,24},{24,32},{32,40},{40,48},{48,56},{56,6... | collective-permute-start | bytes 393224 | tf_op jit(solution)/shard_map/while/body/eval_jaxpr/ppermute | solution.py:12
  33.4 8.4 %collective-permute-start = (bf16[2,256,128]{2,1,0:T(8,128)(2,1)S(1)}, bf16[2,256,128]{2,1,0:T(8,128)(2,1)S(1)}, u32[]{:S(2)}, u32[]{:S(2)}) collective-permute-start(bf16[2,256,128]{2,1,0:T(8,128)(2,1)S(1)} %get-tuple-element.251), channel_id=1, source_target_pairs={{120,0},{0,8},{8,16},{16,24},{24,32},{32,40},{40,48},{48,56},{56,6... | collective-permute-start | bytes 393224 | tf_op jit(solution)/shard_map/while/body/eval_jaxpr/ppermute | solution.py:12
  44.3 8.4 %collective-permute-start = (bf16[2,256,128]{2,1,0:T(8,128)(2,1)S(1)}, bf16[2,256,128]{2,1,0:T(8,128)(2,1)S(1)}, u32[]{:S(2)}, u32[]{:S(2)}) collective-permute-start(bf16[2,256,128]{2,1,0:T(8,128)(2,1)S(1)} %get-tuple-element.251), channel_id=1, source_target_pairs={{120,0},{0,8},{8,16},{16,24},{24,32},{32,40},{40,48},{48,56},{56,6... | collective-permute-start | bytes 393224 | tf_op jit(solution)/shard_map/while/body/eval_jaxpr/ppermute | solution.py:12
  55.3 8.4 %collective-permute-start = (bf16[2,256,128]{2,1,0:T(8,128)(2,1)S(1)}, bf16[2,256,128]{2,1,0:T(8,128)(2,1)S(1)}, u32[]{:S(2)}, u32[]{:S(2)}) collective-permute-start(bf16[2,256,128]{2,1,0:T(8,128)(2,1)S(1)} %get-tuple-element.251), channel_id=1, source_target_pairs={{120,0},{0,8},{8,16},{16,24},{24,32},{32,40},{40,48},{48,56},{56,6... | collective-permute-start | bytes 393224 | tf_op jit(solution)/shard_map/while/body/eval_jaxpr/ppermute | solution.py:12
  66.2 8.4 %collective-permute-start = (bf16[2,256,128]{2,1,0:T(8,128)(2,1)S(1)}, bf16[2,256,128]{2,1,0:T(8,128)(2,1)S(1)}, u32[]{:S(2)}, u32[]{:S(2)}) collective-permute-start(bf16[2,256,128]{2,1,0:T(8,128)(2,1)S(1)} %get-tuple-element.251), channel_id=1, source_target_pairs={{120,0},{0,8},{8,16},{16,24},{24,32},{32,40},{40,48},{48,56},{56,6... | collective-permute-start | bytes 393224 | tf_op jit(solution)/shard_map/while/body/eval_jaxpr/ppermute | solution.py:12
  77.1 8.4 %collective-permute-start = (bf16[2,256,128]{2,1,0:T(8,128)(2,1)S(1)}, bf16[2,256,128]{2,1,0:T(8,128)(2,1)S(1)}, u32[]{:S(2)}, u32[]{:S(2)}) collective-permute-start(bf16[2,256,128]{2,1,0:T(8,128)(2,1)S(1)} %get-tuple-element.251), channel_id=1, source_target_pairs={{120,0},{0,8},{8,16},{16,24},{24,32},{32,40},{40,48},{48,56},{56,6... | collective-permute-start | bytes 393224 | tf_op jit(solution)/shard_map/while/body/eval_jaxpr/ppermute | solution.py:12
  88.0 9.5 %collective-permute-start = (bf16[2,256,128]{2,1,0:T(8,128)(2,1)S(1)}, bf16[2,256,128]{2,1,0:T(8,128)(2,1)S(1)}, u32[]{:S(2)}, u32[]{:S(2)}) collective-permute-start(bf16[2,256,128]{2,1,0:T(8,128)(2,1)S(1)} %get-tuple-element.251), channel_id=1, source_target_pairs={{120,0},{0,8},{8,16},{16,24},{24,32},{32,40},{40,48},{48,56},{56,6... | collective-permute-start | bytes 393224 | tf_op jit(solution)/shard_map/while/body/eval_jaxpr/ppermute | solution.py:12
  100.0 8.9 %collective-permute-start = (bf16[2,256,128]{2,1,0:T(8,128)(2,1)S(1)}, bf16[2,256,128]{2,1,0:T(8,128)(2,1)S(1)}, u32[]{:S(2)}, u32[]{:S(2)}) collective-permute-start(bf16[2,256,128]{2,1,0:T(8,128)(2,1)S(1)} %get-tuple-element.251), channel_id=1, source_target_pairs={{120,0},{0,8},{8,16},{16,24},{24,32},{32,40},{40,48},{48,56},{56,6... | collective-permute-start | bytes 393224 | tf_op jit(solution)/shard_map/while/body/eval_jaxpr/ppermute | solution.py:12
  111.5 8.4 %collective-permute-start = (bf16[2,256,128]{2,1,0:T(8,128)(2,1)S(1)}, bf16[2,256,128]{2,1,0:T(8,128)(2,1)S(1)}, u32[]{:S(2)}, u32[]{:S(2)}) collective-permute-start(bf16[2,256,128]{2,1,0:T(8,128)(2,1)S(1)} %get-tuple-element.251), channel_id=1, source_target_pairs={{120,0},{0,8},{8,16},{16,24},{24,32},{32,40},{40,48},{48,56},{56,6... | collective-permute-start | bytes 393224 | tf_op jit(solution)/shard_map/while/body/eval_jaxpr/ppermute | solution.py:12
  122.4 8.4 %collective-permute-start = (bf16[2,256,128]{2,1,0:T(8,128)(2,1)S(1)}, bf16[2,256,128]{2,1,0:T(8,128)(2,1)S(1)}, u32[]{:S(2)}, u32[]{:S(2)}) collective-permute-start(bf16[2,256,128]{2,1,0:T(8,128)(2,1)S(1)} %get-tuple-element.251), channel_id=1, source_target_pairs={{120,0},{0,8},{8,16},{16,24},{24,32},{32,40},{40,48},{48,56},{56,6... | collective-permute-start | bytes 393224 | tf_op jit(solution)/shard_map/while/body/eval_jaxpr/ppermute | solution.py:12
  133.3 8.4 %collective-permute-start = (bf16[2,256,128]{2,1,0:T(8,128)(2,1)S(1)}, bf16[2,256,128]{2,1,0:T(8,128)(2,1)S(1)}, u32[]{:S(2)}, u32[]{:S(2)}) collective-permute-start(bf16[2,256,128]{2,1,0:T(8,128)(2,1)S(1)} %get-tuple-element.251), channel_id=1, source_target_pairs={{120,0},{0,8},{8,16},{16,24},{24,32},{32,40},{40,48},{48,56},{56,6... | collective-permute-start | bytes 393224 | tf_op jit(solution)/shard_map/while/body/eval_jaxpr/ppermute | solution.py:12
  144.2 8.4 %collective-permute-start = (bf16[2,256,128]{2,1,0:T(8,128)(2,1)S(1)}, bf16[2,256,128]{2,1,0:T(8,128)(2,1)S(1)}, u32[]{:S(2)}, u32[]{:S(2)}) collective-permute-start(bf16[2,256,128]{2,1,0:T(8,128)(2,1)S(1)} %get-tuple-element.251), channel_id=1, source_target_pairs={{120,0},{0,8},{8,16},{16,24},{24,32},{32,40},{40,48},{48,56},{56,6... | collective-permute-start | bytes 393224 | tf_op jit(solution)/shard_map/while/body/eval_jaxpr/ppermute | solution.py:12
  155.1 8.4 %collective-permute-start = (bf16[2,256,128]{2,1,0:T(8,128)(2,1)S(1)}, bf16[2,256,128]{2,1,0:T(8,128)(2,1)S(1)}, u32[]{:S(2)}, u32[]{:S(2)}) collective-permute-start(bf16[2,256,128]{2,1,0:T(8,128)(2,1)S(1)} %get-tuple-element.251), channel_id=1, source_target_pairs={{120,0},{0,8},{8,16},{16,24},{24,32},{32,40},{40,48},{48,56},{56,6... | collective-permute-start | bytes 393224 | tf_op jit(solution)/shard_map/while/body/eval_jaxpr/ppermute | solution.py:12
  166.1 8.4 %collective-permute-start = (bf16[2,256,128]{2,1,0:T(8,128)(2,1)S(1)}, bf16[2,256,128]{2,1,0:T(8,128)(2,1)S(1)}, u32[]{:S(2)}, u32[]{:S(2)}) collective-permute-start(bf16[2,256,128]{2,1,0:T(8,128)(2,1)S(1)} %get-tuple-element.251), channel_id=1, source_target_pairs={{120,0},{0,8},{8,16},{16,24},{24,32},{32,40},{40,48},{48,56},{56,6... | collective-permute-start | bytes 393224 | tf_op jit(solution)/shard_map/while/body/eval_jaxpr/ppermute | solution.py:12
  177.0 8.4 %collective-permute-start = (bf16[2,256,128]{2,1,0:T(8,128)(2,1)S(1)}, bf16[2,256,128]{2,1,0:T(8,128)(2,1)S(1)}, u32[]{:S(2)}, u32[]{:S(2)}) collective-permute-start(bf16[2,256,128]{2,1,0:T(8,128)(2,1)S(1)} %get-tuple-element.251), channel_id=1, source_target_pairs={{120,0},{0,8},{8,16},{16,24},{24,32},{32,40},{40,48},{48,56},{56,6... | collective-permute-start | bytes 393224 | tf_op jit(solution)/shard_map/while/body/eval_jaxpr/ppermute | solution.py:12
Sparse Core Ops, SparseCore 0:
  205.3 35.4 reduce-scatter.1
